TPU v7x, 32 devices: a whole 2x2x4 slice. The times are simulated.
32 devices in a mesh: rows: 4 (over z), chan: 8 (over y, x, core).
Axes of the slice: x: 2, y: 2, z: 4, core: 2. Of those that a mesh axis runs over, the one named last changes fastest.
Arguments:
- feats: bfloat16 [64, 1024, 1024], P('rows', 'chan'), may hold values from -140 to 140
- norm_gain: float32 [1024], P('chan'), may hold values from 0.1 to 1.9
- proj_weight: float32 [8, 1024], P(None, 'chan'), may hold values from -320 to 320
- chan_bias: float32 [1024], P('chan'), may hold values from -8 to -2
Outputs:
- mixed: bfloat16 [64, 1024, 1024], P('rows', 'chan')
All inputs are finite; a program needn't handle non-finite values.
Results may differ from a plain program's by a relative error of at most 0.001.
Values sent between devices are 32-bit elements; how exact they have to be, the bound alone decides.
A program may use at most 128 MiB of HBM per device.

v0:
```python
import jax
import jax.numpy as jnp
from jax import lax
from jax.sharding import PartitionSpec as P

CHANNELS = 1024


EPSILON = 1e-05


def advance(current, row_weights, row_rate):
    edge_zero = jnp.zeros_like(current[:, :1])
    left_side = jnp.concatenate([edge_zero, current[:, :-1]], axis=1)
    right_side = jnp.concatenate([current[:, 1:], edge_zero], axis=1)
    blended = (
        row_weights[0][None, :] * left_side
        + row_weights[1][None, :] * current
        + row_weights[2][None, :] * right_side
    )
    return (1.0 - row_rate) * blended


def coefficients(logits, chan_bias, offset):
    weights = jax.nn.softmax(logits[:, offset : offset + 3, :], axis=1)
    rates = jax.nn.sigmoid(logits[:, 6 + offset // 3, :][:, None, :] + chan_bias[None, :, None])
    return (weights, rates)


def sweep_rows(start, weights, rates, drive, reverse, keep):

    def sweep_row_step(current, inputs):
        row_weights, row_rate, row_drive = inputs
        current = advance(current, row_weights, row_rate) + row_drive
        return (current, current if keep else None)

    return lax.scan(sweep_row_step, start, (weights, rates, drive), reverse=reverse)


def carry_through(start, weights, rates, reverse):

    def carry_row_step(current, inputs):
        return (advance(current, inputs[0], inputs[1]), None)

    finished, _ = lax.scan(carry_row_step, start, (weights, rates), reverse=reverse)
    return finished


def shards(feats, norm_gain, proj_weight, chan_bias):
    logit_scale = CHANNELS ** (-0.5)
    values = feats.astype(jnp.float32)
    squares = jnp.sum(values * values, axis=1)
    square_total = lax.psum(squares, "chan")
    inverse = 1.0 / jnp.sqrt(square_total / CHANNELS + EPSILON)
    normed = values * inverse[:, None, :] * norm_gain[None, :, None]
    projected = jnp.einsum(
        "jc,rcw->rjw",
        proj_weight,
        normed,
        precision=lax.Precision.HIGHEST,
        preferred_element_type=jnp.float32,
    )
    logits = lax.psum(projected, "chan") * logit_scale
    down_weights, down_rate = coefficients(logits, chan_bias, 0)
    up_weights, up_rate = coefficients(logits, chan_bias, 3)
    down_drive = jnp.sqrt(down_rate) * normed
    up_drive = jnp.sqrt(up_rate) * normed
    anchor = jnp.zeros((feats.shape[1], feats.shape[2]), jnp.float32)
    down_local, _ = sweep_rows(anchor, down_weights, down_rate, down_drive, False, False)
    up_local, _ = sweep_rows(anchor, up_weights, up_rate, up_drive, True, False)
    gathered, down_ends, up_ends = (
        lax.all_gather(logits, "rows", axis=0, tiled=True),
        lax.all_gather(down_local, "rows", axis=0, tiled=True),
        lax.all_gather(up_local, "rows", axis=0, tiled=True),
    )
    position = lax.axis_index("rows")
    devices = lax.axis_size("rows")
    block_rows = logits.shape[0]
    local_chans = feats.shape[1]

    def down_visit(visited, current):
        visited = jnp.asarray(visited).astype(jnp.int32)
        block_logits = lax.dynamic_slice_in_dim(gathered, visited * block_rows, block_rows, 0)
        block_weights, block_rates = coefficients(block_logits, chan_bias, 0)
        block_end = lax.dynamic_slice_in_dim(down_ends, visited * local_chans, local_chans, 0)
        return carry_through(current, block_weights, block_rates, False) + block_end

    def up_visit(turn, current):
        visited = (devices - 1 - jnp.asarray(turn)).astype(jnp.int32)
        block_logits = lax.dynamic_slice_in_dim(gathered, visited * block_rows, block_rows, 0)
        block_weights, block_rates = coefficients(block_logits, chan_bias, 3)
        block_end = lax.dynamic_slice_in_dim(up_ends, visited * local_chans, local_chans, 0)
        return carry_through(current, block_weights, block_rates, True) + block_end

    down_in = lax.fori_loop(0, position, down_visit, anchor)
    up_in = lax.fori_loop(0, devices - 1 - position, up_visit, anchor)
    _, down_rows = sweep_rows(down_in, down_weights, down_rate, down_drive, False, True)
    _, up_rows = sweep_rows(up_in, up_weights, up_rate, up_drive, True, True)
    return (down_rows * up_rows).astype(jnp.bfloat16)


def solution(mesh):
    in_specs = (P("rows", "chan", None), P("chan"), P(None, "chan"), P("chan"))
    out_specs = P("rows", "chan", None)
    return jax.shard_map(shards, mesh=mesh, in_specs=in_specs, out_specs=out_specs, check_vma=False)
```

profile of v0, /device:TPU:0, one launch (start us, length us, event | category | flops | bytes accessed | tf_op | source)
XLA Modules:
  0.0 489.4 jit_solution(14477030094933963573)
XLA Ops:
  6.5 3.9 fusion.28
  10.5 56.0 %all-reduce.15.cloned.1.call-done = f32[16,1024]{1,0:T(8,128)} async-done(((f32[16,1024]{1,0:T(8,128)}), f32[16,1024]{1,0:T(8,128)}) %all-reduce.15.cloned.1.call-update) | async-done | bytes 65552 | tf_op jit(solution)/shard_map/psum | solution.py:53
  67.4 7.7 %fusion.36 = f32[16,8,1024]{2,1,0:T(8,128)} fusion(bf16[16,128,1024]{2,1,0:T(8,128)(2,1)} %param.20, f32[128]{0:T(128)} %param.21, f32[16,1024]{1,0:T(8,128)S(1)} %add_rsqrt_fusion, f32[8,128]{1,0:T(8,128)S(1)} %copy-done), kind=kOutput, calls=%fused_computation.76 | convolution fusion | flops 207618048 | bytes 4788736 | tf_op jit(solution)/shard_map/jc,rcw->rjw/dot_general | solution.py:56
  75.1 54.3 %all-reduce.17.cloned.1.call-done = f32[16,8,1024]{2,1,0:T(8,128)} async-done(((f32[16,8,1024]{2,1,0:T(8,128)}), f32[16,8,1024]{2,1,0:T(8,128)}) %all-reduce.17.cloned.1.call-update) | async-done | bytes 524304 | tf_op jit(solution)/shard_map/psum | solution.py:63
  131.1 15.1 %fusion.30 = (f32[16,128,1024]{2,1,0:T(8,128)}, f32[16,128,1024]{2,1,0:T(8,128)}, f32[16,128,1024]{2,1,0:T(8,128)}, f32[16,128,1024]{2,1,0:T(8,128)}) fusion(bf16[16,128,1024]{2,1,0:T(8,128)(2,1)} %param.20, f32[128]{0:T(128)S(1)} %copy-done.6, f32[16,1024]{1,0:T(8,128)S(1)} %add_rsqrt_fusion, f32[128]{0:T(128)S(1)} %copy-done.5, ...), kind=kLoop, calls=%fused_computation.68 | loop fusion | flops 27262976 | bytes 37946368 | tf_op jit(solution)/shard_map/mul | solution.py:67
  146.2 30.4 %while.121 = (s32[]{:T(128)}, f32[128,1024]{1,0:T(8,128)S(1)}, f32[16,128,1024]{2,1,0:T(8,128)}, f32[16,3,1024]{2,1,0:T(4,128)S(1)}, f32[16,128,1024]{2,1,0:T(8,...) while((s32[]{:T(128)}, f32[128,1024]{1,0:T(8,128)S(1)}, ...), condition=%wide.region_18.19_spmd.clone, body=%wide.region_17.18_spmd.clone.sunk | while | flops 1310726 | bytes 6325412 | solution.py:37
  178.1 31.0 %while.120 = (s32[]{:T(128)}, f32[128,1024]{1,0:T(8,128)S(1)}, f32[16,128,1024]{2,1,0:T(8,128)}, f32[16,3,1024]{2,1,0:T(4,128)S(1)}, f32[16,128,1024]{2,1,0:T(8,128)}, /*index=5*/s32[]{:T(128)}, s32[]{:T(128)}, s32[]{}, s32[]{}) while((s32[]{:T(128)}, f32[128,1024]{1,0:T(8,128)S(1)}, f32[16,128,1024]{2,1,0:T(8,128)}, ...), condition=%wide.region_6.0_spmd.clone, body=%wide.region_5.0_spmd.clone.sunk | while | flops 1310725 | bytes 6325392 | solution.py:37
  209.9 12.7 %all-gather.8.cloned.1.call-done = f32[512,1024]{1,0:T(8,128)} async-done(((f32[128,1024]{1,0:T(8,128)}), f32[512,1024]{1,0:T(8,128)}) %all-gather.8.cloned.1.call-update) | async-done | bytes 2097168 | tf_op jit(solution)/shard_map/all_gather | solution.py:74
  222.6 45.9 %all-gather.4.cloned.1.call-done = f32[64,8,1024]{2,1,0:T(8,128)} async-done(((f32[16,8,1024]{2,1,0:T(8,128)}), f32[64,8,1024]{2,1,0:T(8,128)}) %all-gather.4.cloned.1.call-update) | async-done | bytes 2097168 | tf_op jit(solution)/shard_map/all_gather | solution.py:72
  268.6 112.8 %while.118 = (s32[]{:T(128)}, f32[128,1024]{1,0:T(8,128)S(1)}, s32[]{:T(128)}, f32[64,8,1024]{2,1,0:T(8,128)}, f32[128]{0:T(128)S(1)}, /*index=5*/f32[512,1024]{...) while((s32[]{:T(128)}, f32[128,1024]{1,0:T(8,128)S(1)}, ...), condition=%wide.region_24.25_spmd, body=%wide.region_19.24_spmd.sunk | while | flops 9568278 | bytes 15501354 | solution.py:96
  269.9 5.4 %add_divide_fusion.7 = f32[16,128,1024]{2,1,0:T(8,128)} fusion(f32[128]{0:T(128)S(1)} %get-tuple-element.1319, f32[16,1024]{1,0:T(8,128)S(1)} %bitcast.131), kind=kLoop, calls=%fused_computation.30.clone.1 | loop fusion | flops 8388608 | bytes 8454656 | tf_op jit(solution)/shard_map/while/body/div | solution.py:26
  276.8 28.4 %while.123 = (s32[]{:T(128)}, f32[128,1024]{1,0:T(8,128)S(1)}, f32[16,128,1024]{2,1,0:T(8,128)}, f32[16,3,1024]{2,1,0:T(4,128)S(1)}, s32[]{:T(128)}, /*index=5*/s32[]{:T(128)}, s32[]{:T(128)}, s32[]{}, s32[]{}) while((s32[]{:T(128)}, f32[128,1024]{1,0:T(8,128)S(1)}, f32[16,128,1024]{2,1,0:T(8,128)}, f32[16,3,1024]{2,1,0:T(4,128)S(1)}, ...), condition=%wide.region_23.23_spmd, body=%wide.region_22.22_spmd.sunk | while | flops 917509 | bytes 4752529 | solution.py:45
  307.5 5.4 %add_divide_fusion.7 = f32[16,128,1024]{2,1,0:T(8,128)} fusion(f32[128]{0:T(128)S(1)} %get-tuple-element.1319, f32[16,1024]{1,0:T(8,128)S(1)} %bitcast.131), kind=kLoop, calls=%fused_computation.30.clone.1 | loop fusion | flops 8388608 | bytes 8454656 | tf_op jit(solution)/shard_map/while/body/div | solution.py:26
  314.4 28.3 %while.123 = (s32[]{:T(128)}, f32[128,1024]{1,0:T(8,128)S(1)}, f32[16,128,1024]{2,1,0:T(8,128)}, f32[16,3,1024]{2,1,0:T(4,128)S(1)}, s32[]{:T(128)}, /*index=5*/s32[]{:T(128)}, s32[]{:T(128)}, s32[]{}, s32[]{}) while((s32[]{:T(128)}, f32[128,1024]{1,0:T(8,128)S(1)}, f32[16,128,1024]{2,1,0:T(8,128)}, f32[16,3,1024]{2,1,0:T(4,128)S(1)}, ...), condition=%wide.region_23.23_spmd, body=%wide.region_22.22_spmd.sunk | while | flops 917509 | bytes 4752529 | solution.py:45
  345.0 5.4 %add_divide_fusion.7 = f32[16,128,1024]{2,1,0:T(8,128)} fusion(f32[128]{0:T(128)S(1)} %get-tuple-element.1319, f32[16,1024]{1,0:T(8,128)S(1)} %bitcast.131), kind=kLoop, calls=%fused_computation.30.clone.1 | loop fusion | flops 8388608 | bytes 8454656 | tf_op jit(solution)/shard_map/while/body/div | solution.py:26
  351.9 28.3 %while.123 = (s32[]{:T(128)}, f32[128,1024]{1,0:T(8,128)S(1)}, f32[16,128,1024]{2,1,0:T(8,128)}, f32[16,3,1024]{2,1,0:T(4,128)S(1)}, s32[]{:T(128)}, /*index=5*/s32[]{:T(128)}, s32[]{:T(128)}, s32[]{}, s32[]{}) while((s32[]{:T(128)}, f32[128,1024]{1,0:T(8,128)S(1)}, f32[16,128,1024]{2,1,0:T(8,128)}, f32[16,3,1024]{2,1,0:T(4,128)S(1)}, ...), condition=%wide.region_23.23_spmd, body=%wide.region_22.22_spmd.sunk | while | flops 917509 | bytes 4752529 | solution.py:45
  381.4 4.3 broadcast.113.clone.1
  385.6 41.8 %while.119 = (s32[]{:T(128)}, f32[128,1024]{1,0:T(8,128)S(1)}, f32[16,128,1024]{2,1,0:T(8,128)}, f32[16,128,1024]{2,1,0:T(8,128)}, f32[16,3,1024]{2,1,0:T(4,128)...) while((s32[]{:T(128)}, f32[128,1024]{1,0:T(8,128)S(1)}, ...), condition=%wide.region_26.27_spmd, body=%wide.region_25.26_spmd.sunk | while | flops 1048581 | bytes 5801121 | solution.py:37
  385.9 2.4 bitcast_dynamic-update-slice_fusion.5
  388.5 2.4 bitcast_dynamic-update-slice_fusion.5
  391.1 2.4 bitcast_dynamic-update-slice_fusion.5
  393.7 2.4 bitcast_dynamic-update-slice_fusion.5
  396.3 2.4 bitcast_dynamic-update-slice_fusion.5
  401.5 2.4 bitcast_dynamic-update-slice_fusion.5
  404.2 2.4 bitcast_dynamic-update-slice_fusion.5
  409.4 2.4 bitcast_dynamic-update-slice_fusion.5
  412.0 2.4 bitcast_dynamic-update-slice_fusion.5
  414.6 2.4 bitcast_dynamic-update-slice_fusion.5
  419.8 2.4 bitcast_dynamic-update-slice_fusion.5
  422.4 2.4 bitcast_dynamic-update-slice_fusion.5
  425.1 2.4 bitcast_dynamic-update-slice_fusion.5
  427.5 4.3 broadcast.113.clone
  431.8 41.8 %while.116 = (s32[]{:T(128)}, f32[128,1024]{1,0:T(8,128)S(1)}, f32[16,128,1024]{2,1,0:T(8,128)}, f32[16,128,1024]{2,1,0:T(8,128)}, f32[16,3,1024]{2,1,0:T(4,128)...) while((s32[]{:T(128)}, f32[128,1024]{1,0:T(8,128)S(1)}, ...), condition=%wide.region_14.15_spmd, body=%wide.region_13.14_spmd.sunk | while | flops 1048580 | bytes 5801609 | solution.py:37
  432.0 2.4 bitcast_dynamic-update-slice_fusion.4
  434.6 2.4 bitcast_dynamic-update-slice_fusion.4
  437.2 2.4 bitcast_dynamic-update-slice_fusion.4
  442.5 2.4 bitcast_dynamic-update-slice_fusion.4
  445.1 2.4 bitcast_dynamic-update-slice_fusion.4
  447.7 2.4 bitcast_dynamic-update-slice_fusion.4
  452.9 2.4 bitcast_dynamic-update-slice_fusion.4
  455.5 2.4 bitcast_dynamic-update-slice_fusion.4
  458.1 2.4 bitcast_dynamic-update-slice_fusion.4
  460.8 2.4 bitcast_dynamic-update-slice_fusion.4
  463.4 2.4 bitcast_dynamic-update-slice_fusion.4
  466.0 2.4 bitcast_dynamic-update-slice_fusion.4
  468.6 2.4 bitcast_dynamic-update-slice_fusion.4
  471.2 2.4 bitcast_dynamic-update-slice_fusion.4
  473.6 9.3 %multiply_convert_fusion = bf16[16,128,1024]{2,1,0:T(8,128)(2,1)} fusion(f32[16,128,1024]{2,1,0:T(8,128)} %get-tuple-element.568, f32[16,128,1024]{2,1,0:T(8,128)} %get-tuple-element.571), kind=kLoop, calls=%fused_computation.71 | loop fusion | flops 4194304 | bytes 20971520 | tf_op jit(solution)/shard_map/convert_element_type | solution.py:99
  (389 shorter events, 178.6 us)
Async XLA Ops:
  6.5 60.8 %copy-start = (f32[8,128]{1,0:T(8,128)S(1)}, f32[8,128]{1,0:T(8,128)}, u32[]{:S(2)}) copy-start(f32[8,128]{1,0:T(8,128)} %param.22) | copy-start | bytes 12292
  6.5 124.5 %copy-start.6 = (f32[128]{0:T(128)S(1)}, f32[128]{0:T(128)}, u32[]{:S(2)}) copy-start(f32[128]{0:T(128)} %param.21) | copy-start | bytes 1540
  6.5 124.6 %copy-start.5 = (f32[128]{0:T(128)S(1)}, f32[128]{0:T(128)}, u32[]{:S(2)}) copy-start(f32[128]{0:T(128)} %param.23) | copy-start | bytes 1540
  6.5 60.0 %all-reduce.15.cloned.1.call-start = ((), (), s32[]{:S(2)}) async-start(), calls=%async_computation | async-start | bytes 131072 | tf_op jit(solution)/shard_map/psum | solution.py:53
  10.5 119.0 %all-reduce.17.cloned.1.call-start = ((), (), s32[]{:S(2)}) async-start(), calls=%async_computation.1 | async-start | bytes 1048576 | tf_op jit(solution)/shard_map/psum | solution.py:63
  75.1 147.5 %all-gather.8.cloned.1.call-start = ((), (), s32[]{:S(2)}) async-start(), calls=%async_computation.4 | async-start | bytes 2621440 | tf_op jit(solution)/shard_map/all_gather | solution.py:74
  130.5 47.0 %copy-start.4 = (f32[16,8,1024]{2,1,0:T(8,128)}, f32[16,8,1024]{2,1,0:T(8,128)S(1)}, u32[]{:S(2)}) copy-start(f32[16,8,1024]{2,1,0:T(8,128)S(1)} %broadcast_multiply_fusion) | copy-start | bytes 1572868
  176.7 0.8 copy-start.2
  177.5 91.0 %all-gather.4.cloned.1.call-start = ((), (), s32[]{:S(2)}) async-start(), calls=%async_computation.2 | async-start | bytes 2621440 | tf_op jit(solution)/shard_map/all_gather | solution.py:72
  178.1 249.4 %all-gather.6.cloned.1.call-start = ((), (), s32[]{:S(2)}) async-start(), calls=%async_computation.3 | async-start | bytes 2621440 | tf_op jit(solution)/shard_map/all_gather | solution.py:73
  209.1 0.8 copy-start.3
  473.6 9.3 %copy-start.1 = (f32[8,128]{1,0:T(8,128)S(1)}, f32[8,128]{1,0:T(8,128)}, u32[]{:S(2)}) copy-start(f32[8,128]{1,0:T(8,128)} %param.22) | copy-start | bytes 12292
Sparse Core Ops, SparseCore 0:
  10.6 55.8 all-reduce.14
  75.2 54.1 all-reduce.16
  177.6 44.9 all-gather.7
  224.0 44.4 all-gather.3
  269.9 44.4 all-gather.5
where the time goes:
time: 494 us; the launch traced here: 489 us
  other arithmetic  258 us (52%)
  waiting for transfers between devices  169 us (34%)
  local copies, waits for them, and re-layouts  38.3 us (8%)
  between operations  13.3 us (3%)
  matrix products  7.69 us (2%)
    dynamic_update_slice x32, other arithmetic, sweep_rows(): lax.scan(sweep_row_step, start, (weights, rates, drive), reverse=reverse)  76.6 us
    mul x48, other arithmetic, advance(): return (1.0 - row_rate) * blended  73.1 us
    psum x1, waiting for transfers between devices, shards(): square_total = lax.psum(squares, 'chan')  56 us
    psum x1, waiting for transfers between devices, shards(): logits = lax.psum(projected, 'chan') * logit_scale  54.3 us
    add x32, other arithmetic, sweep_row_step(): current = advance(current, row_weights, row_rate) + row_drive  51.8 us
    all_gather x1, waiting for transfers between devices, shards(): lax.all_gather(logits, 'rows', axis=0, tiled=True)  45.9 us
    slice x112, local copies, waits for them, and re-layouts, advance(): left_side = jnp.concatenate([edge_zero, current[:, :-1]], axis=1)  22.6 us
    div x3, other arithmetic, coefficients(): jax.nn.sigmoid(logits[:, 6 + offset // 3, :][:, None, :] + chan_bias[None...  16.3 us
  transfers between devices with their start and end apart: 5, of which 4 were waited for; matrix products, arithmetic and copies ran while one was open for 38% of the time, Pallas kernels for 0%

commit v1 on v0

v1 whole, which is shorter than its diff:
```python
import functools

import jax
import jax.numpy as jnp
from jax import lax
from jax.experimental import pallas as pl
from jax.experimental.pallas import tpu as pltpu
from jax.sharding import PartitionSpec as P

EPSILON = 1e-05
LANES = 128
CHUNK = 16
SKEW = 2
UNROLL = 4


def kernel(
    n_rows, n_chan,
    feats, gain_ref, proj_ref, bias_ref,
    out,
    xv, ov, held, in_d, in_u, out_d, out_u,
    part, core_in, half_sum, pieces, final, wst, fac, gain2,
    row_sem, out_sem, s1_send, s1_recv, s2_send, s2_recv, s3_send, s3_recv, s4_send, s4_recv,
    d_send, d_recv, u_send, u_recv,
):
    height, chans, width = xv.shape
    groups = width // LANES
    tiles = height * groups
    half = tiles // 2
    chips = n_chan // 2
    piece = half // chips
    half_rows = height // 2
    total_chans = chans * n_chan
    row_at = lax.axis_index("rows")
    chan_at = lax.axis_index("chan")
    core = lax.rem(chan_at, 2)
    chip = lax.div(chan_at, 2)
    partner = {"chan": chan_at + 1 - 2 * core}

    def same_core(at):
        return {"chan": lax.rem(at, chips) * 2 + core}

    barrier = pltpu.get_barrier_semaphore()
    MESH = pl.DeviceIdType.MESH

    def load_row(r):
        return pltpu.make_async_copy(feats.at[r], xv.at[r], row_sem.at[r])

    def row_order(i):
        return lax.rem(i + (1 - core) * half_rows, height)

    for i in range(height):
        load_row(row_order(i)).start()
    pl.semaphore_signal(barrier, inc=1, device_id=partner, device_id_type=MESH)
    for d in range(1, chips):
        pl.semaphore_signal(barrier, inc=1, device_id=same_core(chip + d), device_id_type=MESH)

    @pl.when(row_at > 0)
    def _():
        pl.semaphore_signal(barrier, inc=1, device_id={"rows": row_at - 1}, device_id_type=MESH)

    @pl.when(row_at < n_rows - 1)
    def _():
        pl.semaphore_signal(barrier, inc=1, device_id={"rows": row_at + 1}, device_id_type=MESH)

    scaled = proj_ref[...] * (gain_ref[...] * (float(total_chans) ** -0.5))
    wst[...] = jnp.zeros_like(wst)
    wst[0:1, :] = scaled[0:1] - scaled[1:2]
    wst[1:2, :] = scaled[2:3] - scaled[1:2]
    wst[2:3, :] = scaled[3:4] - scaled[4:5]
    wst[3:4, :] = scaled[5:6] - scaled[4:5]
    wst[4:6, :] = scaled[6:8]
    whole = wst[0:8, :]
    high = whole.astype(jnp.bfloat16).astype(jnp.float32)
    rest = whole - high
    middle = rest.astype(jnp.bfloat16).astype(jnp.float32)
    wst[0:8, :] = high
    wst[8:16, :] = middle
    wst[16:24, :] = rest - middle
    lhs = wst[...].astype(jnp.bfloat16)
    fac[...] = jnp.exp(-jnp.transpose(jnp.broadcast_to(bias_ref[...], (LANES, chans))))
    gain_all = jnp.transpose(jnp.broadcast_to(gain_ref[...], (LANES, chans)))
    gain2[...] = gain_all * gain_all

    @pl.when(row_at == 0)
    def _():
        in_d[...] = jnp.zeros_like(in_d)

    @pl.when(row_at == n_rows - 1)
    def _():
        in_u[...] = jnp.zeros_like(in_u)

    waits = chips + (row_at > 0).astype(jnp.int32) + (row_at < n_rows - 1).astype(jnp.int32)
    pl.semaphore_wait(barrier, waits)

    quantity = lax.broadcasted_iota(jnp.int32, (8, width), 0)

    def project(i):
        r = row_order(i)
        load_row(r).wait()
        x = xv[r]
        dots = jnp.dot(lhs, x, preferred_element_type=jnp.float32)
        sums = dots[0:8] + (dots[8:16] + dots[16:24])
        xf = x.astype(jnp.float32)
        squares = jnp.sum(xf * xf, axis=0, keepdims=True)
        sums = jnp.where(quantity == 6, jnp.broadcast_to(squares, sums.shape), sums)
        for k in range(groups):
            part[r * groups + k] = sums[:, k * LANES : (k + 1) * LANES]

    per_row = groups

    def project_send(i, _):
        project(i)
        r = row_order(i)
        pltpu.make_async_remote_copy(
            src_ref=part.at[pl.ds(r * per_row, per_row)],
            dst_ref=core_in.at[pl.ds(i * per_row, per_row)],
            send_sem=s1_send, recv_sem=s1_recv, device_id=partner, device_id_type=MESH,
        ).start()
        return 0

    def project_keep(i, _):
        project(i + half_rows)
        return 0

    lax.fori_loop(0, half_rows, project_send, 0)
    lax.fori_loop(0, half_rows, project_keep, 0)

    whole_half = pltpu.make_async_remote_copy(
        src_ref=part.at[pl.ds((1 - core) * half, half)],
        dst_ref=core_in,
        send_sem=s1_send, recv_sem=s1_recv, device_id=partner, device_id_type=MESH,
    )
    whole_half.wait_recv()

    own_half = core * half

    def scatter_copy(d):
        to = lax.rem(chip + d, chips)
        return pltpu.make_async_remote_copy(
            src_ref=half_sum.at[pl.ds(to * piece, piece)],
            dst_ref=pieces.at[d],
            send_sem=s2_send.at[d], recv_sem=s2_recv.at[d],
            device_id=same_core(chip + d), device_id_type=MESH,
        )

    for d in list(range(1, chips)) + [0]:
        to = lax.rem(chip + d, chips) * piece
        half_sum[pl.ds(to, piece)] = part[pl.ds(own_half + to, piece)] + core_in[pl.ds(to, piece)]
        if d:
            scatter_copy(d).start()
    mine = chip * piece
    summed = half_sum[pl.ds(mine, piece)]
    for d in range(1, chips):
        scatter_copy(d).wait_recv()
        summed = summed + pieces[d]
    pieces[0] = summed

    own = own_half + mine

    def logit(q):
        return pieces[0, :, q, :]

    inverse = lax.rsqrt(logit(6) / total_chans + EPSILON)
    for side in range(2):
        before = logit(2 * side) * inverse
        after = logit(2 * side + 1) * inverse
        top = jnp.maximum(jnp.maximum(before, after), 0.0)
        e_before = jnp.exp(before - top)
        e_after = jnp.exp(after - top)
        scale = 1.0 / (e_before + jnp.exp(-top) + e_after)
        final[pl.ds(own, piece), 2 * side, :] = e_before * scale
        final[pl.ds(own, piece), 2 * side + 1, :] = e_after * scale
        final[pl.ds(own, piece), 4 + side, :] = jnp.exp(-(logit(4 + side) * inverse))
    final[pl.ds(own, piece), 6, :] = inverse
    final[pl.ds(own, piece), 7, :] = inverse

    def gather_copy(d):
        return pltpu.make_async_remote_copy(
            src_ref=final.at[pl.ds(own, piece)],
            dst_ref=final.at[pl.ds(own, piece)],
            send_sem=s3_send.at[d], recv_sem=s3_recv.at[d],
            device_id=same_core(chip + d), device_id_type=MESH,
        )

    def forward_copy(d):
        at = own_half + lax.rem(chip + chips - d, chips) * piece
        return pltpu.make_async_remote_copy(
            src_ref=final.at[pl.ds(at, piece)],
            dst_ref=final.at[pl.ds(at, piece)],
            send_sem=s4_send.at[d], recv_sem=s4_recv.at[d],
            device_id=partner, device_id_type=MESH,
        )

    for d in range(1, chips):
        gather_copy(d).start()
    forward_copy(0).start()
    for d in range(1, chips):
        gather_copy(d).wait_recv()
        forward_copy(d).start()
    for d in range(chips):
        forward_copy(d).wait_recv()

    n_chunks = chans // CHUNK
    lane = lax.broadcasted_iota(jnp.int32, (CHUNK, LANES), 1)
    first_lane = lane == 0
    last_lane = lane == LANES - 1

    def sweep(g, side, second, start_ref, end_ref):
        c0 = pl.multiple_of(g * CHUNK, CHUNK)
        channels = pl.ds(c0, CHUNK)
        factor = fac[channels, :]
        gains = gain2[channels, :]

        def step(i, state):
            r = i if side == 0 else height - 1 - i
            rolled_up = [pltpu.roll(v, 1, 1) for v in state]
            rolled_down = [pltpu.roll(v, LANES - 1, 1) for v in state]
            result = []
            for k in range(groups):
                t = r * groups + k
                cols = pl.ds(k * LANES, LANES)
                a0 = final[t, 2 * side : 2 * side + 1, :]
                a2 = final[t, 2 * side + 1 : 2 * side + 2, :]
                a1 = (1.0 - a0) - a2
                e = final[t, 4 + side : 5 + side, :]
                inv = final[t, 6:7, :]
                left_edge = rolled_up[k - 1] if k else jnp.zeros_like(state[k])
                right_edge = rolled_down[k + 1] if k < groups - 1 else jnp.zeros_like(state[k])
                left = jnp.where(first_lane, left_edge, rolled_up[k])
                right = jnp.where(last_lane, right_edge, rolled_down[k])
                root = lax.rsqrt(1.0 + e * factor)
                drive = root * (xv[r, channels, cols].astype(jnp.float32) * inv)
                v = (1.0 - root * root) * (a0 * left + a1 * state[k] + a2 * right) + drive
                if second:
                    product = held[r, channels, cols] * v * gains
                    ov[r, channels, cols] = product.astype(jnp.bfloat16)
                else:
                    held[r, channels, cols] = v
                result.append(v)
            return tuple(result)

        state = tuple(start_ref[channels, pl.ds(k * LANES, LANES)] for k in range(groups))
        state = lax.fori_loop(0, height, step, state, unroll=UNROLL)
        for k in range(groups):
            end_ref[channels, pl.ds(k * LANES, LANES)] = state[k]

    def pass_copy(g, side):
        channels = pl.ds(pl.multiple_of(g * CHUNK, CHUNK), CHUNK)
        src, dst, send, recv = (
            (out_d, in_d, d_send, d_recv) if side == 0 else (out_u, in_u, u_send, u_recv)
        )
        to = jnp.minimum(row_at + 1, n_rows - 1) if side == 0 else jnp.maximum(row_at - 1, 0)
        return pltpu.make_async_remote_copy(
            src_ref=src.at[channels], dst_ref=dst.at[channels],
            send_sem=send.at[g], recv_sem=recv.at[g],
            device_id={"rows": to}, device_id_type=MESH,
        )

    def store_copy(g):
        channels = pl.ds(pl.multiple_of(g * CHUNK, CHUNK), CHUNK)
        return pltpu.make_async_copy(ov.at[:, channels], out.at[:, channels], out_sem.at[g])

    down_first = row_at < n_rows - 1 - row_at

    def turn(s, _):
        for side in range(2):
            away = row_at if side == 0 else n_rows - 1 - row_at
            g = s - away * SKEW
            start_ref, end_ref = (in_d, out_d) if side == 0 else (in_u, out_u)
            is_first = down_first if side == 0 else jnp.logical_not(down_first)

            @pl.when((g >= 0) & (g < n_chunks))
            def _():
                @pl.when(away > 0)
                def _():
                    pass_copy(g, side).wait_recv()

                @pl.when(is_first)
                def _():
                    sweep(g, side, False, start_ref, end_ref)

                @pl.when(jnp.logical_not(is_first))
                def _():
                    sweep(g, side, True, start_ref, end_ref)

                @pl.when(away < n_rows - 1)
                def _():
                    pass_copy(g, side).start()

                @pl.when(jnp.logical_not(is_first))
                def _():
                    store_copy(g).start()

        return 0

    lax.fori_loop(0, n_chunks + (n_rows - 1) * SKEW, turn, 0)

    whole_half.wait_send()
    for d in range(1, chips):
        scatter_copy(d).wait_send()
        gather_copy(d).wait_send()
    for d in range(chips):
        forward_copy(d).wait_send()
    for g in range(n_chunks):
        store_copy(g).wait()

        @pl.when(row_at < n_rows - 1)
        def _():
            pass_copy(g, 0).wait_send()

        @pl.when(row_at > 0)
        def _():
            pass_copy(g, 1).wait_send()


def shards(n_rows, n_chan, feats, norm_gain, proj_weight, chan_bias):
    height, chans, width = feats.shape
    tiles = height * width // LANES
    half = tiles // 2
    chips = n_chan // 2
    piece = half // chips
    n_chunks = chans // CHUNK
    f32 = jnp.float32
    dma = pltpu.SemaphoreType.DMA
    vmem = pl.BlockSpec(memory_space=pltpu.VMEM)
    return pl.pallas_call(
        functools.partial(kernel, n_rows, n_chan),
        out_shape=jax.ShapeDtypeStruct(feats.shape, jnp.bfloat16),
        in_specs=[pl.BlockSpec(memory_space=pl.ANY), vmem, vmem, vmem],
        out_specs=pl.BlockSpec(memory_space=pl.ANY),
        scratch_shapes=[
            pltpu.VMEM(feats.shape, jnp.bfloat16),
            pltpu.VMEM(feats.shape, jnp.bfloat16),
            pltpu.VMEM(feats.shape, f32),
        ]
        + [pltpu.VMEM((chans, width), f32)] * 4
        + [
            pltpu.VMEM((tiles, 8, LANES), f32),
            pltpu.VMEM((half, 8, LANES), f32),
            pltpu.VMEM((half, 8, LANES), f32),
            pltpu.VMEM((chips, piece, 8, LANES), f32),
            pltpu.VMEM((tiles, 8, LANES), f32),
            pltpu.VMEM((32, chans), f32),
            pltpu.VMEM((chans, LANES), f32),
            pltpu.VMEM((chans, LANES), f32),
            dma((height,)), dma((n_chunks,)),
            dma, dma,
            dma((chips,)), dma((chips,)), dma((chips,)), dma((chips,)), dma((chips,)), dma((chips,)),
            dma((n_chunks,)), dma((n_chunks,)), dma((n_chunks,)), dma((n_chunks,)),
        ],
        compiler_params=pltpu.CompilerParams(
            collective_id=0, has_side_effects=True, vmem_limit_bytes=60 * 1024 * 1024
        ),
        name="propagate",
    )(feats, norm_gain.reshape(1, chans), proj_weight, chan_bias.reshape(1, chans))


def solution(mesh):
    in_specs = (P("rows", "chan", None), P("chan"), P(None, "chan"), P("chan"))
    out_specs = P("rows", "chan", None)
    body = functools.partial(shards, mesh.shape["rows"], mesh.shape["chan"])
    return jax.shard_map(body, mesh=mesh, in_specs=in_specs, out_specs=out_specs, check_vma=False)
```

time: 494 us -> 62.8 us (0.13)
  other arithmetic: 258 us -> 0 us
  waiting for transfers between devices: 169 us -> 0 us
  Pallas kernels: 0 us -> 57.8 us
  local copies, waits for them, and re-layouts: 38.3 us -> 4.81 us
  between operations: 13.3 us -> 0.01 us
  matrix products: 7.69 us -> 0 us
    psum x2 -> x0, waiting for transfers between devices: 110 us -> none  [the longest x1 56 us: shards(): square_total = lax.psum(squares, 'chan')]
    mul x50 -> x0, other arithmetic: 89.3 us -> none  [the longest x48 73.1 us: advance(): return (1.0 - row_rate) * blended]
    dynamic_update_slice x32 -> x0, other arithmetic: 76.6 us -> none  [sweep_rows(): lax.scan(sweep_row_step, start, (weights, rates, drive), reverse=reverse)]
    all_gather x3 -> x0, waiting for transfers between devices: 58.6 us -> none  [the longest x1 45.9 us: shards(): lax.all_gather(logits, 'rows', axis=0, tiled=True)]
    pallas_call x0 -> x1, Pallas kernels: none -> 57.8 us  [shards(): pl.pallas_call(functools.partial(kernel, n_rows, n_chan), out_shape=jax.S...]
    add x35 -> x0, other arithmetic: 55.3 us -> none  [the longest x32 51.8 us: sweep_row_step(): current = advance(current, row_weights, row_rate) + row_drive]
    slice x228 -> x0, local copies, waits for them, and re-layouts: 28 us -> none  [the longest x112 22.6 us: advance(): left_side = jnp.concatenate([edge_zero, current[:, :-1]], axis=1)]
    div x8 -> x0, other arithmetic: 21.3 us -> none  [the longest x3 16.3 us: coefficients(): jax.nn.sigmoid(logits[:, 6 + offset // 3, :][:, None, :] + chan_bias[None...]
  transfers between devices with their start and end apart: 5 -> 0, of which waited for: 4 -> 0; matrix products, arithmetic and copies ran while one was open for 38% -> 0% of each run, Pallas kernels for 0% -> 0%
where the time goes in v1:
time: 62.8 us; the launch traced here: 62.6 us
  Pallas kernels  57.8 us (92%)
  local copies, waits for them, and re-layouts  4.81 us (8%)
    pallas_call x1, Pallas kernels, shards(): pl.pallas_call(functools.partial(kernel, n_rows, n_chan), out_shape=jax.S...  57.8 us
    unnamed x1, local copies, waits for them, and re-layouts  4.81 us

profile of v1, /device:TPU:0, one launch (start us, length us, event | category | flops | bytes accessed | tf_op | source)
XLA Modules:
  0.0 62.6 jit_solution(4842216772550682384)
XLA Ops:
  0.0 57.8 %propagate.1 = bf16[16,128,1024]{2,1,0:T(8,128)(2,1)} custom-call(bf16[16,128,1024]{2,1,0:T(8,128)(2,1)} %feats.1, f32[1,128]{1,0:T(1,128)} %bitcast.2, f32[8,128]{1,0:T(8,128)} %proj_ref.1, f32[1,128]{1,0:T(1,128)} %bitcast.3), custom_call_target="tpu_custom_call" | custom-call | tf_op jit(solution)/shard_map/propagate/pallas_call | solution.py:327
  57.8 4.8 %copy.6 = bf16[16,128,1024]{2,1,0:T(8,128)(2,1)} copy(bf16[16,128,1024]{2,1,0:T(8,128)(2,1)} %propagate.1) | data formatting | bytes 8388608

commit v2 on v1

--- a/solution.py
+++ b/solution.py
@@ -9,7 +9,7 @@
 
 EPSILON = 1e-05
 LANES = 128
-CHUNK = 16
+CHUNK = 32
 SKEW = 2
 UNROLL = 4
 
@@ -17,10 +17,10 @@
 def kernel(
     n_rows, n_chan,
     feats, gain_ref, proj_ref, bias_ref,
-    out,
-    xv, ov, held, in_d, in_u, out_d, out_u,
+    ov,
+    xv, held, in_d, in_u, out_d, out_u,
     part, core_in, half_sum, pieces, final, wst, fac, gain2,
-    row_sem, out_sem, s1_send, s1_recv, s2_send, s2_recv, s3_send, s3_recv, s4_send, s4_recv,
+    row_sem, s1_send, s1_recv, s2_send, s2_recv, s3_send, s3_recv, s4_send, s4_recv,
     d_send, d_recv, u_send, u_recv,
 ):
     height, chans, width = xv.shape
@@ -170,10 +170,11 @@
         e_after = jnp.exp(after - top)
         scale = 1.0 / (e_before + jnp.exp(-top) + e_after)
         final[pl.ds(own, piece), 2 * side, :] = e_before * scale
+        if side == 0:
+            final[pl.ds(own, piece), 7, :] = jnp.exp(-top) * scale
         final[pl.ds(own, piece), 2 * side + 1, :] = e_after * scale
         final[pl.ds(own, piece), 4 + side, :] = jnp.exp(-(logit(4 + side) * inverse))
     final[pl.ds(own, piece), 6, :] = inverse
-    final[pl.ds(own, piece), 7, :] = inverse
 
     def gather_copy(d):
         return pltpu.make_async_remote_copy(
@@ -205,6 +206,9 @@
     lane = lax.broadcasted_iota(jnp.int32, (CHUNK, LANES), 1)
     first_lane = lane == 0
     last_lane = lane == LANES - 1
+
+    def weight(t, q):
+        return final[t, pl.ds(q, 8, stride=0), :]
 
     def sweep(g, side, second, start_ref, end_ref):
         c0 = pl.multiple_of(g * CHUNK, CHUNK)
@@ -220,18 +224,21 @@
             for k in range(groups):
                 t = r * groups + k
                 cols = pl.ds(k * LANES, LANES)
-                a0 = final[t, 2 * side : 2 * side + 1, :]
-                a2 = final[t, 2 * side + 1 : 2 * side + 2, :]
-                a1 = (1.0 - a0) - a2
-                e = final[t, 4 + side : 5 + side, :]
-                inv = final[t, 6:7, :]
+                a0 = weight(t, 2 * side)
+                a2 = weight(t, 2 * side + 1)
+                a1 = (1.0 - a0) - a2 if side else weight(t, 7)
+                a0, a1, a2, e, inv = (
+                    jnp.concatenate([one] * (CHUNK // 8), axis=0)
+                    for one in (a0, a1, a2, weight(t, 4 + side), weight(t, 6))
+                )
                 left_edge = rolled_up[k - 1] if k else jnp.zeros_like(state[k])
                 right_edge = rolled_down[k + 1] if k < groups - 1 else jnp.zeros_like(state[k])
                 left = jnp.where(first_lane, left_edge, rolled_up[k])
                 right = jnp.where(last_lane, right_edge, rolled_down[k])
                 root = lax.rsqrt(1.0 + e * factor)
-                drive = root * (xv[r, channels, cols].astype(jnp.float32) * inv)
-                v = (1.0 - root * root) * (a0 * left + a1 * state[k] + a2 * right) + drive
+                normed = xv[r, channels, cols].astype(jnp.float32) * inv
+                blended = a0 * left + a1 * state[k] + a2 * right
+                v = blended + root * (normed - root * blended)
                 if second:
                     product = held[r, channels, cols] * v * gains
                     ov[r, channels, cols] = product.astype(jnp.bfloat16)
@@ -257,10 +264,6 @@
             device_id={"rows": to}, device_id_type=MESH,
         )
 
-    def store_copy(g):
-        channels = pl.ds(pl.multiple_of(g * CHUNK, CHUNK), CHUNK)
-        return pltpu.make_async_copy(ov.at[:, channels], out.at[:, channels], out_sem.at[g])
-
     down_first = row_at < n_rows - 1 - row_at
 
     def turn(s, _):
@@ -288,10 +291,6 @@
                 def _():
                     pass_copy(g, side).start()
 
-                @pl.when(jnp.logical_not(is_first))
-                def _():
-                    store_copy(g).start()
-
         return 0
 
     lax.fori_loop(0, n_chunks + (n_rows - 1) * SKEW, turn, 0)
@@ -303,8 +302,6 @@
     for d in range(chips):
         forward_copy(d).wait_send()
     for g in range(n_chunks):
-        store_copy(g).wait()
-
         @pl.when(row_at < n_rows - 1)
         def _():
             pass_copy(g, 0).wait_send()
@@ -326,11 +323,10 @@
     vmem = pl.BlockSpec(memory_space=pltpu.VMEM)
     return pl.pallas_call(
         functools.partial(kernel, n_rows, n_chan),
-        out_shape=jax.ShapeDtypeStruct(feats.shape, jnp.bfloat16),
+        out_shape=pltpu.VMEM(feats.shape, jnp.bfloat16),
         in_specs=[pl.BlockSpec(memory_space=pl.ANY), vmem, vmem, vmem],
-        out_specs=pl.BlockSpec(memory_space=pl.ANY),
+        out_specs=pl.BlockSpec(memory_space=pltpu.VMEM),
         scratch_shapes=[
-            pltpu.VMEM(feats.shape, jnp.bfloat16),
             pltpu.VMEM(feats.shape, jnp.bfloat16),
             pltpu.VMEM(feats.shape, f32),
         ]
@@ -344,13 +340,13 @@
             pltpu.VMEM((32, chans), f32),
             pltpu.VMEM((chans, LANES), f32),
             pltpu.VMEM((chans, LANES), f32),
-            dma((height,)), dma((n_chunks,)),
+            dma((height,)),
             dma, dma,
             dma((chips,)), dma((chips,)), dma((chips,)), dma((chips,)), dma((chips,)), dma((chips,)),
             dma((n_chunks,)), dma((n_chunks,)), dma((n_chunks,)), dma((n_chunks,)),
         ],
         compiler_params=pltpu.CompilerParams(
-            collective_id=0, has_side_effects=True, vmem_limit_bytes=60 * 1024 * 1024
+            collective_id=0, has_side_effects=True, vmem_limit_bytes=56 * 1024 * 1024
         ),
         name="propagate",
     )(feats, norm_gain.reshape(1, chans), proj_weight, chan_bias.reshape(1, chans))

time: 62.8 us -> 55.1 us (0.88)
  Pallas kernels: 57.8 us -> 52.9 us
  local copies, waits for them, and re-layouts: 4.81 us -> 2.02 us
    pallas_call x1, Pallas kernels: 57.8 us -> 52.9 us  [shards(): pl.pallas_call(functools.partial(kernel, n_rows, n_chan), out_shape=pltpu...]
    unnamed x1, local copies, waits for them, and re-layouts: 4.81 us -> 2.02 us
where the time goes in v2:
time: 55.1 us; the launch traced here: 54.9 us
  Pallas kernels  52.9 us (96%)
  local copies, waits for them, and re-layouts  2.02 us (4%)
    pallas_call x1, Pallas kernels, shards(): pl.pallas_call(functools.partial(kernel, n_rows, n_chan), out_shape=pltpu...  52.9 us
    unnamed x1, local copies, waits for them, and re-layouts  2.02 us

profile of v2, /device:TPU:0, one launch (start us, length us, event | category | flops | bytes accessed | tf_op | source)
XLA Modules:
  0.0 54.9 jit_solution(7684206521895205305)
XLA Ops:
  0.0 52.9 %propagate.1 = bf16[16,128,1024]{2,1,0:T(8,128)(2,1)S(1)} custom-call(bf16[16,128,1024]{2,1,0:T(8,128)(2,1)} %feats.1, f32[1,128]{1,0:T(1,128)} %bitcast.2, f32[8,128]{1,0:T(8,128)} %proj_ref.1, f32[1,128]{1,0:T(1,128)} %bitcast.3), custom_call_target="tpu_custom_call" | custom-call | tf_op jit(solution)/shard_map/propagate/pallas_call | solution.py:324
  52.9 2.0 %copy.6 = bf16[16,128,1024]{2,1,0:T(8,128)(2,1)} copy(bf16[16,128,1024]{2,1,0:T(8,128)(2,1)S(1)} %propagate.1) | data formatting | bytes 8388608
